TPU v7x, 128 devices: a whole 4x4x4 slice. The times are simulated.
128 devices in a mesh: ray: 16 (over x, z), tile: 8 (over y, core).
Axes of the slice: x: 4, y: 4, z: 4, core: 2. Of those that a mesh axis runs over, the one named last changes fastest.
Arguments:
- data: float32 [64, 262144], P(None, ('ray', 'tile')), may hold values from -6 to 6
- sensitivity: bfloat16 [4096, 256, 512], P(('ray', 'tile')), may hold values from -0.25 to 0.25
- block_tiles: int32 [128, 8, 4], P(('ray', 'tile')), may hold values from 0 to 47
- block_bundles: int32 [128, 8, 4], P(('ray', 'tile')), may hold values from 0 to 7
Outputs:
- solution: float32 [64, 196608], P(None, 'tile')
- residual: float32 [64, 262144], P(None, ('ray', 'tile'))
Inputs may be any that keep to these rules, and one draw needn't show every extreme that they name: `block_tiles`: position of the block's tile among the 48 tiles of the owner given by the second index. `block_bundles`: the block's ray bundle among the device's 8 bundles.
All inputs are finite; a program needn't handle non-finite values.
Results may differ from a plain program's by a relative error of at most 0.004.
The roundings to bfloat16 on the way count: a program that leaves them out, or rounds other values in their place, can miss the bound.
Values may be sent and summed in bfloat16 or wider, within the bound.
A program may use at most 128 MiB of HBM per device.

v0:
```python
import jax
import jax.numpy as jnp
from jax import lax
from jax.sharding import PartitionSpec as P

RB = 256
CB = 512
ITERS = 2
BUND_DEV = 8
TILE_DEV = 48
eps_norm = 1e-06


def per_device(data, sensitivity, block_tiles, block_bundles):
    columns = data.shape[0]
    bundles = block_bundles.reshape(-1)
    requests = lax.all_to_all(block_tiles, "tile", split_axis=1, concat_axis=1, tiled=True).reshape(
        -1
    )
    bundle_onehot = (bundles[:, None] == jnp.arange(BUND_DEV, dtype=jnp.int32)[None, :]).astype(
        jnp.float32
    )
    owner_onehot = (requests[:, None] == jnp.arange(TILE_DEV, dtype=jnp.int32)[None, :]).astype(
        jnp.bfloat16
    )

    def fetch(field_bf):
        owned = field_bf.reshape(columns, TILE_DEV, CB)
        outgoing = jnp.take(owned, requests, axis=1)
        tiles = lax.all_to_all(outgoing, "tile", split_axis=1, concat_axis=1, tiled=True)
        return tiles

    def forward(field_bf):
        tiles = fetch(field_bf)
        partial_value = jnp.einsum(
            "cnk,nrk->ncr", tiles, sensitivity, preferred_element_type=jnp.float32
        )
        summed = jnp.einsum(
            "ncr,nb->cbr", partial_value, bundle_onehot, precision=lax.Precision.HIGHEST
        )
        return summed.reshape(columns, BUND_DEV * RB)

    def adjoint(rays_bf):
        picked = jnp.take(rays_bf.reshape(columns, BUND_DEV, RB), bundles, axis=1)
        terms = jnp.einsum(
            "cnr,nrk->cnk", picked, sensitivity, preferred_element_type=jnp.float32
        ).astype(jnp.bfloat16)
        arrived = lax.all_to_all(terms, "tile", split_axis=1, concat_axis=1, tiled=True)
        owned = jnp.einsum(
            "cnk,nt->ctk", arrived, owner_onehot, preferred_element_type=jnp.float32
        ).reshape(columns, TILE_DEV * CB)
        total = lax.psum(owned, "ray")
        return total

    def cell_norm(field):
        local = jnp.sum(field * field, axis=1)
        total = lax.psum(local, "tile")
        return jnp.sqrt(total + eps_norm)

    def ray_norm(rays):
        total = lax.psum(jnp.sum(rays * rays, axis=1), ("ray", "tile"))
        return jnp.sqrt(total + eps_norm)

    beta_now = ray_norm(data)
    rays_dir = data / beta_now[:, None]
    model_dir = adjoint(rays_dir.astype(jnp.bfloat16))
    alpha_now = cell_norm(model_dir)
    model_dir = model_dir / alpha_now[:, None]
    search = model_dir
    solution = jnp.zeros_like(model_dir)
    phi_bar = beta_now
    rho_bar = alpha_now
    for step in range(ITERS):
        rounded = model_dir.astype(jnp.bfloat16)
        rays_dir = forward(rounded) - alpha_now[:, None] * rays_dir
        beta_now = ray_norm(rays_dir)
        rays_dir = rays_dir / beta_now[:, None]
        rho_now = jnp.sqrt(rho_bar * rho_bar + beta_now * beta_now)
        cosine = rho_bar / rho_now
        sine_part = beta_now / rho_now
        phi_now = cosine * phi_bar
        phi_bar = sine_part * phi_bar
        solution = solution + (phi_now / rho_now)[:, None] * search
        if step + 1 < ITERS:
            model_dir = adjoint(rays_dir.astype(jnp.bfloat16)) - beta_now[:, None] * model_dir
            alpha_now = cell_norm(model_dir)
            model_dir = model_dir / alpha_now[:, None]
            theta_now = sine_part * alpha_now
            rho_bar = -cosine * alpha_now
            search = model_dir - (theta_now / rho_now)[:, None] * search
    residual = data - forward(solution.astype(jnp.bfloat16))
    return (solution, residual)


def solution(mesh):
    return jax.shard_map(
        per_device,
        mesh=mesh,
        in_specs=(
            P(None, ("ray", "tile")),
            P(("ray", "tile"), None, None),
            P(("ray", "tile"), None, None),
            P(("ray", "tile"), None, None),
        ),
        out_specs=(P(None, "tile"), P(None, ("ray", "tile"))),
        check_vma=False,
    )
```

profile of v0, /device:TPU:1, one launch (start us, length us, event | category | flops | bytes accessed | tf_op | source)
XLA Modules:
  0.0 731.6 jit_solution(17410393598439722855)
XLA Ops:
  7.2 1.3 copy.22
  8.5 6.0 all-to-all-start
  14.5 0.8 copy.23
  15.2 0.1 reshape.58
  15.3 1.2 multiply_reduce_fusion.4
  16.5 67.7 %psum.49 = f32[64]{0:T(128)S(1)} all-reduce(f32[64]{0:T(128)S(1)} %multiply_reduce_fusion.4), channel_id=1, replica_groups=mesh['ray'=16,'tile'=8] {'ray','tile'}, use_global_device_ids=true, to_apply=%region_1.0 | all-reduce | flops 64 | bytes 512 | tf_op jit(solution)/shard_map/psum | solution.py:61
  84.3 1.1 fusion.19
  85.5 0.6 gather_fusion
  86.1 6.3 convert_bitcast_fusion.1
  92.4 0.0 all-to-all-done
  92.4 4.4 all-to-all-start.1
  96.8 0.5 broadcast.102
  97.3 0.7 reduce.3
  98.0 0.1 eq.28
  98.1 25.1 %all-to-all-done.1 = bf16[64,32,512]{2,0,1:T(8,128)(2,1)S(1)} async-done(((bf16[64,32,512]{2,0,1:T(8,128)(2,1)}), bf16[64,32,512]{2,0,1:T(8,128)(2,1)S(1)}, u32[]{:S(2)}, u32[]{:S(2)}) %all-to-all-start.1) | async-done | bytes 2097184 | tf_op jit(solution)/shard_map/all_to_all | solution.py:48
  123.1 1.7 fusion.8
  124.9 6.3 copy.39
  131.2 0.0 all-reduce.3.cloned.1.call-update
  131.2 0.0 all-reduce.5.cloned.1.call-start
  131.3 119.1 %all-reduce.3.cloned.1.call-done = f32[64,24576]{1,0:T(8,128)} async-done(((f32[64,24576]{1,0:T(8,128)}), f32[64,24576]{1,0:T(8,128)}) %all-reduce.3.cloned.1.call-update) | async-done | bytes 6291472 | tf_op jit(solution)/shard_map/psum | solution.py:52
  250.4 3.3 multiply_reduce_fusion.1
  253.7 12.4 %psum.51 = f32[64]{0:T(128)S(1)} all-reduce(f32[64]{0:T(128)S(1)} %multiply_reduce_fusion.1), channel_id=1, replica_groups=mesh['ray'=16,'tile'=8] {'tile'}, use_global_device_ids=true, to_apply=%region_4.6 | all-reduce | flops 64 | bytes 512 | tf_op jit(solution)/shard_map/psum | solution.py:57
  266.1 3.2 fusion.37
  269.4 0.4 copy.61
  269.8 2.0 gather_fusion.1
  271.8 1.8 select_bitcast_fusion.2
  273.7 31.7 %all_to_all.30 = bf16[64,32,512]{2,0,1:T(8,128)(2,1)S(1)} all-to-all(bf16[64,32,512]{2,0,1:T(8,128)(2,1)S(1)} %select_bitcast_fusion.2), channel_id=1, replica_groups=mesh['ray'=16,'tile'=8] {'tile'}, dimensions={1} | all-to-all | bytes 4194304 | tf_op jit(solution)/shard_map/all_to_all | solution.py:30
  305.4 6.0 fusion.41
  311.4 0.0 copy-start
  311.5 2.0 fusion.6
  313.4 0.2 copy.40
  313.6 0.3 multiply_reduce_fusion.3
  313.9 64.5 %psum.52 = f32[64]{0:T(128)S(1)} all-reduce(f32[64]{0:T(128)S(1)} %get-tuple-element.11), channel_id=1, replica_groups=mesh['ray'=16,'tile'=8] {'ray','tile'}, use_global_device_ids=true, to_apply=%region_6.0 | all-reduce | flops 64 | bytes 512 | tf_op jit(solution)/shard_map/psum | solution.py:61
  378.4 0.1 fusion.20
  378.6 0.6 gather_fusion.2
  379.2 5.0 convert_bitcast_fusion
  384.2 30.1 %all_to_all.31 = bf16[64,32,512]{2,0,1:T(8,128)(2,1)S(1)} all-to-all(bf16[64,32,512]{2,0,1:T(8,128)(2,1)S(1)} %convert_bitcast_fusion), channel_id=1, replica_groups=mesh['ray'=16,'tile'=8] {'tile'}, dimensions={1} | all-to-all | bytes 4194304 | tf_op jit(solution)/shard_map/all_to_all | solution.py:48
  414.3 1.7 fusion.4
  416.0 6.3 copy.41
  422.3 0.0 all-reduce.5.cloned.1.call-update
  422.3 118.9 %all-reduce.5.cloned.1.call-done = f32[64,24576]{1,0:T(8,128)} async-done(((f32[64,24576]{1,0:T(8,128)}), f32[64,24576]{1,0:T(8,128)}) %all-reduce.5.cloned.1.call-update) | async-done | bytes 6291472 | tf_op jit(solution)/shard_map/psum | solution.py:52
  541.2 5.8 multiply_reduce_fusion
  547.0 12.4 %psum.54 = f32[64]{0:T(128)S(1)} all-reduce(f32[64]{0:T(128)S(1)} %multiply_reduce_fusion), channel_id=1, replica_groups=mesh['ray'=16,'tile'=8] {'tile'}, use_global_device_ids=true, to_apply=%region_9.12 | all-reduce | flops 64 | bytes 512 | tf_op jit(solution)/shard_map/psum | solution.py:57
  559.4 5.2 fusion.10
  564.6 0.4 copy.60
  565.1 2.0 gather_fusion.3
  567.1 1.8 select_bitcast_fusion.1
  568.9 31.7 %all_to_all.32 = bf16[64,32,512]{2,0,1:T(8,128)(2,1)S(1)} all-to-all(bf16[64,32,512]{2,0,1:T(8,128)(2,1)S(1)} %select_bitcast_fusion.1), channel_id=1, replica_groups=mesh['ray'=16,'tile'=8] {'tile'}, dimensions={1} | all-to-all | bytes 4194304 | tf_op jit(solution)/shard_map/all_to_all | solution.py:30
  600.7 6.0 fusion.42
  606.7 0.0 copy-start.3
  606.7 2.0 fusion.2
  608.7 0.2 copy.42
  608.9 0.3 multiply_reduce_fusion.2
  609.1 64.8 %psum.55 = f32[64]{0:T(128)S(1)} all-reduce(f32[64]{0:T(128)S(1)} %multiply_reduce_fusion.2), channel_id=1, replica_groups=mesh['ray'=16,'tile'=8] {'ray','tile'}, use_global_device_ids=true, to_apply=%region_11.14 | all-reduce | flops 64 | bytes 512 | tf_op jit(solution)/shard_map/psum | solution.py:61
  673.9 7.4 %fusion.38 = (bf16[64,24576]{1,0:T(8,128)(2,1)S(1)}, f32[64,24576]{1,0:T(8,128)}) fusion(f32[64]{0:T(128)S(1)} %multiply_divide_fusion, f32[64]{0:T(128)S(1)} %add_sqrt_fusion, f32[64,24576]{1,0:T(8,128)} %all-reduce.5.cloned.1.call-done, f32[64]{0:T(128)S(1)} %get-tuple-element.13, f32[64]{0:T(128)S(1)} %get-tuple-element.9, ...), kind=kLoop, calls=%fused_computation.76 | loop fusion | flops 15728640 | bytes 22021632 | tf_op jit(solution)/shard_map/convert_element_type | solution.py:91
  681.3 0.4 copy.59
  681.7 2.0 gather_fusion.4
  683.7 1.8 select_bitcast_fusion
  685.6 30.1 %all_to_all.33 = bf16[64,32,512]{2,0,1:T(8,128)(2,1)S(1)} all-to-all(bf16[64,32,512]{2,0,1:T(8,128)(2,1)S(1)} %select_bitcast_fusion), channel_id=1, replica_groups=mesh['ray'=16,'tile'=8] {'tile'}, dimensions={1} | all-to-all | bytes 4194304 | tf_op jit(solution)/shard_map/all_to_all | solution.py:30
  715.7 6.0 fusion.43
  721.7 0.0 copy-start.1
  721.8 2.0 fusion
  723.7 0.2 copy.43
  723.9 0.9 sub.19
  (20 shorter events, 0.2 us)
Async XLA Ops:
  8.5 83.9 %all-to-all-start = ((s32[1,8,4]{2,0,1:T(1,128)}), s32[1,8,4]{2,0,1:T(1,128)S(1)}, u32[]{:S(2)}, u32[]{:S(2)}) async-start(s32[1,8,4]{2,0,1:T(1,128)} %copy.22), calls=%async_computation | async-start | bytes 8192 | tf_op jit(solution)/shard_map/all_to_all | solution.py:17
  92.4 30.8 %all-to-all-start.1 = ((bf16[64,32,512]{2,0,1:T(8,128)(2,1)}), bf16[64,32,512]{2,0,1:T(8,128)(2,1)S(1)}, u32[]{:S(2)}, u32[]{:S(2)}) async-start(bf16[64,32,512]{2,0,1:T(8,128)(2,1)} %convert_bitcast_fusion.1), calls=%async_computation.1 | async-start | bytes 4194304 | tf_op jit(solution)/shard_map/all_to_all | solution.py:48
  96.8 153.6 %all-reduce.3.cloned.1.call-start = ((), (), s32[]{:S(2)}) async-start(), calls=%async_computation.6 | async-start | bytes 12582912 | tf_op jit(solution)/shard_map/psum | solution.py:52
  131.2 410.0 %all-reduce.5.cloned.1.call-start = ((), (), s32[]{:S(2)}) async-start(), calls=%async_computation.7 | async-start | bytes 12582912 | tf_op jit(solution)/shard_map/psum | solution.py:52
  311.4 2.1 copy-start
  313.9 64.7 %copy-start.2 = (f32[64,2048]{1,0:T(8,128)}, f32[64,2048]{1,0:T(8,128)S(1)}, u32[]{:S(2)}) copy-start(f32[64,2048]{1,0:T(8,128)S(1)} %get-tuple-element.12) | copy-start | bytes 1572868
  606.7 2.1 copy-start.3
  721.7 2.1 copy-start.1
Sparse Core Ops, SparseCore 0:
  131.3 119.0 all-reduce.2
  422.4 118.6 all-reduce.4
where the time goes:
time: 733 us; the launch traced here: 732 us
  blocking collectives  346 us (47%)
  waiting for transfers between devices  263 us (36%)
  matrix products  38.8 us (5%)
  other arithmetic  35 us (5%)
  local copies, waits for them, and re-layouts  24.4 us (3%)
  between operations  14.3 us (2%)
  starting transfers between devices  10.4 us (1%)
    psum x2, waiting for transfers between devices, adjoint(): total = lax.psum(owned, 'ray')  238 us
    psum x3, blocking collectives, ray_norm(): total = lax.psum(jnp.sum(rays * rays, axis=1), ('ray', 'tile'))  197 us
    all_to_all x3, blocking collectives, fetch(): lax.all_to_all(outgoing, 'tile', split_axis=1, concat_axis=1, tiled=True)  93.6 us
    all_to_all x1, blocking collectives, adjoint(): lax.all_to_all(terms, 'tile', split_axis=1, concat_axis=1, tiled=True)  30.1 us
    all_to_all x1, waiting for transfers between devices, adjoint(): lax.all_to_all(terms, 'tile', split_axis=1, concat_axis=1, tiled=True)  25.1 us
    psum x2, blocking collectives, cell_norm(): total = lax.psum(local, 'tile')  24.9 us
    dot_general x3, matrix products, forward(): jnp.einsum('cnk,nrk->ncr', tiles, sensitivity, preferred_element_type=jnp...  18.1 us
    unnamed x15, local copies, waits for them, and re-layouts  15.1 us
  transfers between devices with their start and end apart: 4, of which 3 were waited for; matrix products, arithmetic and copies ran while one was open for 2% of the time, Pallas kernels for 0%

commit v1 on v0

--- a/solution.py
+++ b/solution.py
@@ -58,7 +58,7 @@
         return jnp.sqrt(total + eps_norm)
 
     def ray_norm(rays):
-        total = lax.psum(jnp.sum(rays * rays, axis=1), ("ray", "tile"))
+        total = lax.psum(lax.psum(jnp.sum(rays * rays, axis=1), "ray"), "tile")
         return jnp.sqrt(total + eps_norm)
 
     beta_now = ray_norm(data)

time: 733 us -> 687 us (0.937)
  blocking collectives: 346 us -> 304 us
    psum x3 -> x6, blocking collectives: 197 us -> 156 us  [ray_norm(): total = lax.psum(lax.psum(jnp.sum(rays * rays, axis=1), 'ray'), 'tile')]
where the time goes in v1:
time: 687 us; the launch traced here: 686 us
  blocking collectives  304 us (44%)
  waiting for transfers between devices  259 us (38%)
  matrix products  38.8 us (6%)
  other arithmetic  35 us (5%)
  local copies, waits for them, and re-layouts  24.3 us (4%)
  between operations  14.3 us (2%)
  starting transfers between devices  9.77 us (1%)
    psum x2, waiting for transfers between devices, adjoint(): total = lax.psum(owned, 'ray')  234 us
    psum x6, blocking collectives, ray_norm(): total = lax.psum(lax.psum(jnp.sum(rays * rays, axis=1), 'ray'), 'tile')  156 us
    all_to_all x3, blocking collectives, fetch(): lax.all_to_all(outgoing, 'tile', split_axis=1, concat_axis=1, tiled=True)  93 us
    all_to_all x1, blocking collectives, adjoint(): lax.all_to_all(terms, 'tile', split_axis=1, concat_axis=1, tiled=True)  29.6 us
    psum x2, blocking collectives, cell_norm(): total = lax.psum(local, 'tile')  25.1 us
    all_to_all x1, waiting for transfers between devices, adjoint(): lax.all_to_all(terms, 'tile', split_axis=1, concat_axis=1, tiled=True)  25.1 us
    dot_general x3, matrix products, forward(): jnp.einsum('cnk,nrk->ncr', tiles, sensitivity, preferred_element_type=jnp...  18.1 us
    unnamed x15, local copies, waits for them, and re-layouts  15.1 us
  transfers between devices with their start and end apart: 4, of which 3 were waited for; matrix products, arithmetic and copies ran while one was open for 2% of the time, Pallas kernels for 0%

profile of v1, /device:TPU:1, one launch (start us, length us, event | category | flops | bytes accessed | tf_op | source)
XLA Modules:
  0.0 685.5 jit_solution(15481982511001852928)
XLA Ops:
  7.2 1.3 copy.22
  8.5 6.0 all-to-all-start
  14.5 0.8 copy.23
  15.2 0.1 reshape.58
  15.3 1.2 multiply_reduce_fusion.4
  16.5 34.8 %psum.70 = f32[64]{0:T(128)S(1)} all-reduce(f32[64]{0:T(128)S(1)} %multiply_reduce_fusion.4), channel_id=1, replica_groups=mesh['ray'=16,'tile'=8] {'ray'}, use_global_device_ids=true, to_apply=%region_1.0 | all-reduce | flops 64 | bytes 512 | tf_op jit(solution)/shard_map/psum | solution.py:61
  51.3 19.1 %psum.71 = f32[64]{0:T(128)S(1)} all-reduce(f32[64]{0:T(128)S(1)} %psum.70), channel_id=1, replica_groups=mesh['ray'=16,'tile'=8] {'tile'}, use_global_device_ids=true, to_apply=%region_2.0 | all-reduce | flops 64 | bytes 512 | tf_op jit(solution)/shard_map/psum | solution.py:61
  70.4 1.1 fusion.19
  71.6 0.6 gather_fusion
  72.2 6.3 convert_bitcast_fusion.1
  78.5 3.8 all-to-all-start.1
  82.3 0.5 broadcast.102
  82.8 0.7 reduce.3
  83.4 0.1 eq.28
  83.5 25.1 %all-to-all-done.1 = bf16[64,32,512]{2,0,1:T(8,128)(2,1)S(1)} async-done(((bf16[64,32,512]{2,0,1:T(8,128)(2,1)}), bf16[64,32,512]{2,0,1:T(8,128)(2,1)S(1)}, u32[]{:S(2)}, u32[]{:S(2)}) %all-to-all-start.1) | async-done | bytes 2097184 | tf_op jit(solution)/shard_map/all_to_all | solution.py:48
  108.6 1.7 fusion.8
  110.4 6.3 copy.39
  116.6 0.0 all-reduce.3.cloned.1.call-update
  116.6 0.0 all-reduce.5.cloned.1.call-start
  116.7 117.1 %all-reduce.3.cloned.1.call-done = f32[64,24576]{1,0:T(8,128)} async-done(((f32[64,24576]{1,0:T(8,128)}), f32[64,24576]{1,0:T(8,128)}) %all-reduce.3.cloned.1.call-update) | async-done | bytes 6291472 | tf_op jit(solution)/shard_map/psum | solution.py:52
  233.8 3.3 multiply_reduce_fusion.1
  237.1 12.4 %psum.73 = f32[64]{0:T(128)S(1)} all-reduce(f32[64]{0:T(128)S(1)} %multiply_reduce_fusion.1), channel_id=1, replica_groups=mesh['ray'=16,'tile'=8] {'tile'}, use_global_device_ids=true, to_apply=%region_5.7 | all-reduce | flops 64 | bytes 512 | tf_op jit(solution)/shard_map/psum | solution.py:57
  249.6 3.2 fusion.37
  252.8 0.4 copy.61
  253.3 2.0 gather_fusion.1
  255.3 1.8 select_bitcast_fusion.2
  257.1 31.7 %all_to_all.30 = bf16[64,32,512]{2,0,1:T(8,128)(2,1)S(1)} all-to-all(bf16[64,32,512]{2,0,1:T(8,128)(2,1)S(1)} %select_bitcast_fusion.2), channel_id=1, replica_groups=mesh['ray'=16,'tile'=8] {'tile'}, dimensions={1} | all-to-all | bytes 4194304 | tf_op jit(solution)/shard_map/all_to_all | solution.py:30
  288.8 6.0 fusion.41
  294.9 2.0 fusion.6
  296.9 0.2 copy.40
  297.0 0.3 multiply_reduce_fusion.3
  297.3 31.1 %psum.74 = f32[64]{0:T(128)S(1)} all-reduce(f32[64]{0:T(128)S(1)} %get-tuple-element.11), channel_id=1, replica_groups=mesh['ray'=16,'tile'=8] {'ray'}, use_global_device_ids=true, to_apply=%region_7.0 | all-reduce | flops 64 | bytes 512 | tf_op jit(solution)/shard_map/psum | solution.py:61
  328.4 20.0 %psum.75 = f32[64]{0:T(128)S(1)} all-reduce(f32[64]{0:T(128)S(1)} %psum.74), channel_id=1, replica_groups=mesh['ray'=16,'tile'=8] {'tile'}, use_global_device_ids=true, to_apply=%region_8.11 | all-reduce | flops 64 | bytes 512 | tf_op jit(solution)/shard_map/psum | solution.py:61
  348.5 0.1 fusion.20
  348.6 0.6 gather_fusion.2
  349.2 5.0 convert_bitcast_fusion
  354.2 29.6 %all_to_all.31 = bf16[64,32,512]{2,0,1:T(8,128)(2,1)S(1)} all-to-all(bf16[64,32,512]{2,0,1:T(8,128)(2,1)S(1)} %convert_bitcast_fusion), channel_id=1, replica_groups=mesh['ray'=16,'tile'=8] {'tile'}, dimensions={1} | all-to-all | bytes 4194304 | tf_op jit(solution)/shard_map/all_to_all | solution.py:48
  383.8 1.7 fusion.4
  385.5 6.3 copy.41
  391.8 0.0 all-reduce.5.cloned.1.call-update
  391.8 117.2 %all-reduce.5.cloned.1.call-done = f32[64,24576]{1,0:T(8,128)} async-done(((f32[64,24576]{1,0:T(8,128)}), f32[64,24576]{1,0:T(8,128)}) %all-reduce.5.cloned.1.call-update) | async-done | bytes 6291472 | tf_op jit(solution)/shard_map/psum | solution.py:52
  509.0 5.8 multiply_reduce_fusion
  514.8 12.7 %psum.77 = f32[64]{0:T(128)S(1)} all-reduce(f32[64]{0:T(128)S(1)} %multiply_reduce_fusion), channel_id=1, replica_groups=mesh['ray'=16,'tile'=8] {'tile'}, use_global_device_ids=true, to_apply=%region_11.14 | all-reduce | flops 64 | bytes 512 | tf_op jit(solution)/shard_map/psum | solution.py:57
  527.5 5.2 fusion.10
  532.7 0.4 copy.60
  533.2 2.0 gather_fusion.3
  535.2 1.8 select_bitcast_fusion.1
  537.0 31.7 %all_to_all.32 = bf16[64,32,512]{2,0,1:T(8,128)(2,1)S(1)} all-to-all(bf16[64,32,512]{2,0,1:T(8,128)(2,1)S(1)} %select_bitcast_fusion.1), channel_id=1, replica_groups=mesh['ray'=16,'tile'=8] {'tile'}, dimensions={1} | all-to-all | bytes 4194304 | tf_op jit(solution)/shard_map/all_to_all | solution.py:30
  568.8 6.0 fusion.42
  574.8 0.0 copy-start.3
  574.8 2.0 fusion.2
  576.8 0.2 copy.42
  577.0 0.3 multiply_reduce_fusion.2
  577.2 31.1 %psum.78 = f32[64]{0:T(128)S(1)} all-reduce(f32[64]{0:T(128)S(1)} %multiply_reduce_fusion.2), channel_id=1, replica_groups=mesh['ray'=16,'tile'=8] {'ray'}, use_global_device_ids=true, to_apply=%region_13.16 | all-reduce | flops 64 | bytes 512 | tf_op jit(solution)/shard_map/psum | solution.py:61
  608.3 20.0 %psum.79 = f32[64]{0:T(128)S(1)} all-reduce(f32[64]{0:T(128)S(1)} %psum.78), channel_id=1, replica_groups=mesh['ray'=16,'tile'=8] {'tile'}, use_global_device_ids=true, to_apply=%region_14.17 | all-reduce | flops 64 | bytes 512 | tf_op jit(solution)/shard_map/psum | solution.py:61
  628.4 7.4 %fusion.38 = (bf16[64,24576]{1,0:T(8,128)(2,1)S(1)}, f32[64,24576]{1,0:T(8,128)}) fusion(f32[64]{0:T(128)S(1)} %multiply_divide_fusion, f32[64]{0:T(128)S(1)} %add_sqrt_fusion, f32[64,24576]{1,0:T(8,128)} %all-reduce.5.cloned.1.call-done, f32[64]{0:T(128)S(1)} %get-tuple-element.13, f32[64]{0:T(128)S(1)} %get-tuple-element.9, ...), kind=kLoop, calls=%fused_computation.76 | loop fusion | flops 15728640 | bytes 22021632 | tf_op jit(solution)/shard_map/convert_element_type | solution.py:91
  635.8 0.4 copy.59
  636.2 2.0 gather_fusion.4
  638.2 1.8 select_bitcast_fusion
  640.1 29.6 %all_to_all.33 = bf16[64,32,512]{2,0,1:T(8,128)(2,1)S(1)} all-to-all(bf16[64,32,512]{2,0,1:T(8,128)(2,1)S(1)} %select_bitcast_fusion), channel_id=1, replica_groups=mesh['ray'=16,'tile'=8] {'tile'}, dimensions={1} | all-to-all | bytes 4194304 | tf_op jit(solution)/shard_map/all_to_all | solution.py:30
  669.6 6.0 fusion.43
  675.7 2.0 fusion
  677.6 0.2 copy.43
  677.8 0.9 sub.19
  (23 shorter events, 0.2 us)
Async XLA Ops:
  8.5 70.0 %all-to-all-start = ((s32[1,8,4]{2,0,1:T(1,128)}), s32[1,8,4]{2,0,1:T(1,128)S(1)}, u32[]{:S(2)}, u32[]{:S(2)}) async-start(s32[1,8,4]{2,0,1:T(1,128)} %copy.22), calls=%async_computation | async-start | bytes 8192 | tf_op jit(solution)/shard_map/all_to_all | solution.py:17
  78.5 30.1 %all-to-all-start.1 = ((bf16[64,32,512]{2,0,1:T(8,128)(2,1)}), bf16[64,32,512]{2,0,1:T(8,128)(2,1)S(1)}, u32[]{:S(2)}, u32[]{:S(2)}) async-start(bf16[64,32,512]{2,0,1:T(8,128)(2,1)} %convert_bitcast_fusion.1), calls=%async_computation.1 | async-start | bytes 4194304 | tf_op jit(solution)/shard_map/all_to_all | solution.py:48
  82.3 151.6 %all-reduce.3.cloned.1.call-start = ((), (), s32[]{:S(2)}) async-start(), calls=%async_computation.6 | async-start | bytes 12582912 | tf_op jit(solution)/shard_map/psum | solution.py:52
  116.6 392.4 %all-reduce.5.cloned.1.call-start = ((), (), s32[]{:S(2)}) async-start(), calls=%async_computation.7 | async-start | bytes 12582912 | tf_op jit(solution)/shard_map/psum | solution.py:52
  294.9 2.1 copy-start
  297.3 51.3 %copy-start.2 = (f32[64,2048]{1,0:T(8,128)}, f32[64,2048]{1,0:T(8,128)S(1)}, u32[]{:S(2)}) copy-start(f32[64,2048]{1,0:T(8,128)S(1)} %get-tuple-element.12) | copy-start | bytes 1572868
  574.8 2.1 copy-start.3
  675.7 2.1 copy-start.1
Sparse Core Ops, SparseCore 0:
  116.8 117.0 all-reduce.2
  392.0 117.0 all-reduce.4
